TPU v7x, 512 devices: a whole 4x8x8 slice. The times are simulated.
512 devices in a mesh: slab: 16 (over y, core), tile: 32 (over x, z).
Axes of the slice: x: 4, y: 8, z: 8, core: 2. Of those that a mesh axis runs over, the one named last changes fastest.
Arguments:
- particles: float32 [8, 1048576], P(None, ('slab', 'tile')), may hold values from -6 to 6, as said below
- halo_up: int32 [512], P(('slab', 'tile')), may hold values from 0 to 15
- halo_down: int32 [512], P(('slab', 'tile')), may hold values from 0 to 15
- tile_first: int32 [16, 4096], P('slab', 'tile'), may hold values from 0 to 511, as said below
- tile_second: int32 [16, 4096], P('slab', 'tile'), may hold values from 0 to 575
- tile_live: int32 [16, 4096], P('slab', 'tile'), may hold values from 0 to 1, as said below
- step_index: int32 [1], replicated, may hold values from 0 to 63
- time_step: float32 [1], replicated, may hold values from 0.05 to 0.5
Outputs:
- rates: float32 [4, 1048576], P(None, ('slab', 'tile'))
- advanced: float32 [7, 1048576], P(None, ('slab', 'tile'))
Inputs may be any that keep to these rules, and one draw needn't show every extreme that they name: `particles`: densities lie between 0.85 and 1.15, masses between 0.0002 and 0.0008, positions between 0 and 3. `tile_first`: in each slab the 16 blocks of each device of the slab are named by exactly 128 of the slab's slots. `tile_live`: in each slab exactly half of the 4096 slots are live; how many fall on one device varies.
All inputs are finite; a program needn't handle non-finite values.
Results may differ from a plain program's by a relative error of at most 0.00018.
Values sent between devices are 32-bit elements; how exact they have to be, the bound alone decides.
A program may use at most 64 MiB of HBM per device.

v0:
```python
import heapq
import itertools

import jax
import jax.numpy as jnp
from jax import lax
from jax.experimental import pallas as pl
from jax.experimental.pallas import tpu as pltpu
from jax.sharding import PartitionSpec as P

PB = 128
BLK_DEV = 16
N_SLAB = 16
X, Z = 4, 8
N_TILE = X * Z
CHUNK = BLK_DEV + 2

SMOOTHING = 1.0
KERNEL_NORM = 21.0 / (16.0 * 3.141592653589793)
SOUND_SPEED = 10.0
STIFFNESS = SOUND_SPEED * SOUND_SPEED / 7.0
VISCOSITY = 0.1
BLAST_STRENGTH = 8.0
DECAY_TIME = 8.0

MESH = pl.DeviceIdType.MESH

PARTS = (
    dict(first="z", x2="+", z4="+", lo=0, hi=0, at=0.0),
    dict(first="z", x2="+", z4="+", lo=0, hi=6, at=0.1),
    dict(first="x", x2="+", z4="+", lo=6, hi=10, at=0.1),
    dict(first="z", x2="-", z4="-", lo=10, hi=15, at=0.2),
    dict(first="x", x2="-", z4="-", lo=15, hi=18, at=2.0),
)
BLOCK_US = 4096 / 46.5e3
HOP_US = 1.66


def tree(part):
    x_from = {1: (0, "x+"), 3: (0, "x-"), 2: (1, "x+") if part["x2"] == "+" else (3, "x-")}
    z_from = {1: (0, "z+"), 2: (1, "z+"), 3: (2, "z+"), 7: (0, "z-"), 6: (7, "z-"), 5: (6, "z-")}
    z_from[4] = (3, "z+") if part["z4"] == "+" else (5, "z-")
    children = {}
    for dx, dz in itertools.product(range(X), range(Z)):
        if (dx, dz) == (0, 0):
            continue
        along_z = dz != 0 if part["first"] == "x" else dx == 0
        if along_z:
            parent, way = (dx, z_from[dz][0]), z_from[dz][1]
        else:
            parent, way = (x_from[dx][0], dz), x_from[dx][1]
        children.setdefault(parent, []).append((way, (dx, dz)))
    return children


def schedule():
    trees = [tree(part) for part in PARTS]

    def depth(index, node):
        return max([0] + [1 + depth(index, child) for _, child in trees[index].get(node, [])])

    free = {"x+": 0.0, "x-": 0.0, "z+": 0.0, "z-": 0.0}
    ticket = itertools.count()
    events = [(part["at"], next(ticket), index, (0, 0)) for index, part in enumerate(PARTS)]
    heapq.heapify(events)
    steps = []
    while events:
        now, _, index, node = heapq.heappop(events)
        sends = sorted(trees[index].get(node, []), key=lambda item: -depth(index, item[1]))
        steps.append((index, node, sends))
        blocks = PARTS[index]["hi"] - PARTS[index]["lo"] or 0.5
        for way, child in sends:
            done = max(now, free[way]) + blocks * BLOCK_US
            free[way] = done
            heapq.heappush(events, (done + HOP_US, next(ticket), index, child))
    return steps


STEPS = schedule()


def gather_kernel(up_ref, down_ref, first_ref, second_ref, live_ref, mine_ref,
                  all_ref, lists_ref,
                  own, rim, slots, tiles, slots_sem, own_sem, place_sem, tiles_sem, rim_send, rim_recv, send_sem, recv_sem):
    slab = lax.axis_index("slab")
    tile = lax.axis_index("tile")
    x, z = tile // Z, tile % Z
    above = lax.rem(slab + 1, N_SLAB)
    below = lax.rem(slab + N_SLAB - 1, N_SLAB)
    beside = {
        "x+": lax.rem(x + 1, X) * Z + z,
        "x-": lax.rem(x + X - 1, X) * Z + z,
        "z+": x * Z + lax.rem(z + 1, Z),
        "z-": x * Z + lax.rem(z + Z - 1, Z),
    }
    load = pltpu.make_async_copy(mine_ref, own, own_sem)
    load.start()
    fetch = [
        pltpu.make_async_copy(ref, slots.at[place], slots_sem.at[place])
        for place, ref in enumerate((first_ref, second_ref, live_ref))
    ]
    for copy in fetch:
        copy.start()
    barrier = pltpu.get_barrier_semaphore()
    for way in beside:
        pl.semaphore_signal(barrier, inc=1, device_id=(slab, beside[way]), device_id_type=MESH)
    pl.semaphore_signal(barrier, inc=1, device_id=(above, tile), device_id_type=MESH)
    pl.semaphore_signal(barrier, inc=1, device_id=(below, tile), device_id_type=MESH)
    for copy in fetch:
        copy.wait()
    tiles[...] = jnp.concatenate([slots[0], slots[1], slots[2], jnp.zeros((1, PB), jnp.int32)], axis=0)
    load.wait()
    rim[0] = own[up_ref[0]]
    rim[1] = own[down_ref[0]]
    place = pltpu.make_async_copy(own, all_ref.at[tile, pl.ds(0, BLK_DEV)], place_sem)
    place.start()
    mark = pltpu.make_async_copy(tiles, lists_ref.at[tile], tiles_sem)
    mark.start()
    pl.semaphore_wait(barrier, 6)

    def rim_copy(side):
        return pltpu.make_async_remote_copy(
            src_ref=rim.at[side],
            dst_ref=all_ref.at[tile, BLK_DEV + side],
            send_sem=rim_send.at[side],
            recv_sem=rim_recv.at[side],
            device_id=(above if side == 0 else below, tile),
            device_id_type=MESH,
        )

    rims = [rim_copy(0), rim_copy(1)]
    for copy in rims:
        copy.start()
    place.wait()
    mark.wait()

    def piece(index, node):
        origin = lax.rem(x + X - node[0], X) * Z + lax.rem(z + Z - node[1], Z)
        if index == 0:
            return lists_ref.at[origin]
        part = PARTS[index]
        return all_ref.at[origin, pl.ds(part["lo"], part["hi"] - part["lo"])]

    def slot(index, node):
        return index * N_TILE + node[0] * Z + node[1]

    sent = []
    for index, node, sends in STEPS:
        held = piece(index, node)
        if node != (0, 0):
            pltpu.make_async_remote_copy(
                src_ref=held,
                dst_ref=held,
                send_sem=send_sem.at[slot(index, node)],
                recv_sem=recv_sem.at[slot(index, node)],
                device_id=(slab, beside["x+"]),
                device_id_type=MESH,
            ).wait_recv()
        elif PARTS[index]["hi"] > BLK_DEV:
            for copy in rims:
                copy.wait_recv()
        for way, child in sends:
            copy = pltpu.make_async_remote_copy(
                src_ref=held,
                dst_ref=held,
                send_sem=send_sem.at[slot(index, child)],
                recv_sem=recv_sem.at[slot(index, child)],
                device_id=(slab, beside[way]),
                device_id_type=MESH,
            )
            copy.start()
            sent.append(copy)
    for copy in rims:
        copy.wait_send()
    for copy in sent:
        copy.wait_send()


def gather(halo_up, halo_down, tile_first, tile_second, tile_live, mine):
    smem = pl.BlockSpec(memory_space=pltpu.SMEM)
    hbm = pl.BlockSpec(memory_space=pltpu.HBM)
    anywhere = pl.BlockSpec(memory_space=pl.ANY)
    slots = len(PARTS) * N_TILE
    return pl.pallas_call(
        gather_kernel,
        out_shape=(
            jax.ShapeDtypeStruct((N_TILE, CHUNK, 8, PB), jnp.float32),
            jax.ShapeDtypeStruct((N_TILE, 4, PB), jnp.int32),
        ),
        in_specs=[smem, smem, hbm, hbm, hbm, hbm],
        out_specs=(anywhere, anywhere),
        scratch_shapes=[
            pltpu.VMEM((BLK_DEV, 8, PB), jnp.float32),
            pltpu.VMEM((2, 8, PB), jnp.float32),
            pltpu.VMEM((3, 1, PB), jnp.int32),
            pltpu.VMEM((4, PB), jnp.int32),
            pltpu.SemaphoreType.DMA((3,)),
            pltpu.SemaphoreType.DMA,
            pltpu.SemaphoreType.DMA,
            pltpu.SemaphoreType.DMA,
            pltpu.SemaphoreType.DMA((2,)),
            pltpu.SemaphoreType.DMA((2,)),
            pltpu.SemaphoreType.DMA((slots,)),
            pltpu.SemaphoreType.DMA((slots,)),
        ],
        compiler_params=pltpu.CompilerParams(collective_id=0, has_side_effects=True, vmem_limit_bytes=4 * 2**20),
        name="gather_blocks",
    )(halo_up, halo_down, tile_first, tile_second, tile_live, mine)


def iota(shape, axis):
    return lax.broadcasted_iota(jnp.int32, shape, axis)


def choose_tiles(lists, slab, tile):
    first, second, live = lists[:, 0, :], lists[:, 1, :], lists[:, 2, :]
    missing = ((slab == 0) & (second >= 512) & (second < 544)) | ((slab == N_SLAB - 1) & (second >= 544))
    wanted = ((first >> 4) == tile) & (live == 1) & jnp.logical_not(missing)
    source = jnp.where(
        second < 512,
        (second >> 4) * CHUNK + (second & 15),
        ((second - 512) & 31) * CHUNK + BLK_DEV + ((second - 512) >> 5),
    )
    code = ((first & 15) * 1024 + source).astype(jnp.float32)
    ones = jnp.where(wanted, 1.0, 0.0)
    upto = (iota((PB, PB), 0) <= iota((PB, PB), 1)).astype(jnp.float32)
    within = jnp.dot(ones, upto, preferred_element_type=jnp.float32)
    earlier = (iota((N_TILE, N_TILE), 1) < iota((N_TILE, N_TILE), 0)).astype(jnp.float32)
    before = jnp.dot(earlier, within, preferred_element_type=jnp.float32)[:, PB - 1 :]
    place = jnp.where(wanted, (before + within).astype(jnp.int32) - 1, -1)
    target = iota((PB, PB), 0)
    chosen = jnp.zeros((PB, PB), jnp.float32)
    for row in range(N_TILE):
        chosen = chosen + jnp.where(place[row : row + 1, :] == target, code[row : row + 1, :], 0.0)
    codes = lax.dot_general(
        jnp.ones((8, PB), jnp.float32), chosen, (((1,), (1,)), ((), ())),
        precision=lax.Precision.HIGHEST, preferred_element_type=jnp.float32,
    )
    count = jnp.sum(before[N_TILE - 1 :, :] + within[N_TILE - 1 :, PB - 1 :])
    return jnp.where(iota((8, PB), 0) == 0, codes, count).astype(jnp.int32)


def shifted(rows, up):
    return pltpu.roll(rows, (8 - up) % 8, 0)


def parts_of(value):
    high = value.astype(jnp.bfloat16).astype(jnp.float32)
    rest = value - high
    middle = rest.astype(jnp.bfloat16).astype(jnp.float32)
    return high, middle, rest - middle


def squares_and_products(centred):
    squares = centred * centred
    products = centred * shifted(centred, 3)
    return (
        squares + shifted(squares, 1) + shifted(squares, 2),
        products + shifted(products, 1) + shifted(products, 2),
    )


def pressure_term(density):
    squared = density * density
    return STIFFNESS * (squared * squared * squared * density - 1.0) / squared


def receiver(fields, row):
    centre = jnp.where(row < 6, jnp.broadcast_to(fields[:, 0:1], (8, PB)), 0.0)
    centred = fields - centre
    squares, products = squares_and_products(centred)
    plain = jnp.where(row < 6, centred, jnp.where(row == 6, 1.0, 0.0))
    high, middle, low = parts_of(plain)
    extra = jnp.zeros((8, PB), jnp.float32)
    for place, value in enumerate(parts_of(squares) + parts_of(products)):
        extra = jnp.where(row == place, value if place == 0 else shifted(value, 8 - place), extra)
    pressure = pressure_term(fields)
    columns = jnp.where(row == 0, shifted(pressure, 6), jnp.where(row == 1, shifted(-0.5 * fields, 5), 0.0))
    return centre, jnp.concatenate([high, high, middle, middle, high, low, extra, columns], axis=0).T


def actor_side(centred, row):
    squares, products = squares_and_products(centred)
    for_square = jnp.where(row < 3, -2.0 * centred, jnp.where(row == 6, shifted(squares, 2), 0.0))
    for_approach = jnp.where(
        row < 3, -shifted(centred, 3), jnp.where(row < 6, -shifted(centred, 5), jnp.where(row == 6, shifted(products, 2), 0.0))
    )
    sides = []
    for value, ones in ((for_square, row < 3), (for_approach, (row >= 3) & (row < 6))):
        high, middle, low = parts_of(value)
        extra = jnp.where(ones, 1.0, 0.0)
        sides.append(
            jnp.concatenate([high, middle, high, middle, low, high, extra, jnp.zeros((8, PB), jnp.float32)], axis=0)
        )
    return jnp.concatenate(sides, axis=1).astype(jnp.bfloat16)


NO_TILE = BLK_DEV * 1024
TOGETHER = 2


def rates_kernel(step_ref, length_ref, lists_ref, all_ref, rates_ref, ahead_ref,
                 centre, left, push, rho, total, codes, right, squares, factor, moment, plan, plan_sem):
    slab = lax.axis_index("slab")
    tile = lax.axis_index("tile")
    row = iota((8, PB), 0)
    codes[...] = choose_tiles(lists_ref[...], slab, tile)
    copy = pltpu.make_async_copy(codes, plan, plan_sem)
    copy.start()
    total[...] = jnp.zeros_like(total)

    def one_block(block, carry):
        middle, side = receiver(all_ref[tile * CHUNK + block], row)
        centre[block] = middle
        left[block] = side.astype(jnp.bfloat16)
        push[block] = jnp.broadcast_to(side[:, 56:57], (PB, PB))
        rho[block] = jnp.broadcast_to(side[:, 57:58], (PB, PB))
        return carry

    lax.fori_loop(0, BLK_DEV, one_block, 0)
    copy.wait()
    number = plan[1, 0]

    def code_of(k):
        code = plan[0, jnp.clip(k, 0, PB - 1)]
        return jnp.where((k >= 0) & (k < number), code, NO_TILE)

    def prepare(k, slot):
        code = code_of(k)
        right[slot] = actor_side(all_ref[code & 1023] - centre[code >> 10], row)

    def first_product(k, slot):
        squares[slot] = jnp.dot(left[code_of(k) >> 10], right[slot], preferred_element_type=jnp.float32)

    def elementwise(k, slot):
        code = code_of(k)
        a = code >> 10
        fields = all_ref[code & 1023]
        centred = fields - centre[a]
        act_push = jnp.broadcast_to(pressure_term(fields)[6:7], (16, PB))
        act_rho = jnp.broadcast_to(-0.5 * fields[6:7], (16, PB))
        mass = jnp.broadcast_to(fields[7:8] * (5.0 * KERNEL_NORM / 8.0), (8, PB))
        weighted = jnp.where(row == 0, 1.0, shifted(centred, 7)) * mass
        high = weighted.astype(jnp.bfloat16).astype(jnp.float32)
        both = jnp.where(row < 4, high, shifted(weighted - high, 4))
        both = jnp.concatenate([both, jnp.zeros((8, PB), jnp.float32)], axis=0).astype(jnp.bfloat16)
        moment[slot] = jnp.concatenate([both, both], axis=1)
        for low in range(0, PB, 16):
            rows = pl.ds(low, 16)
            dist_sq = jnp.maximum(squares[slot, rows, 0:PB], 1e-30)
            approach = squares[slot, rows, PB : 2 * PB]
            reach = jnp.maximum(2.0 - dist_sq * lax.rsqrt(dist_sq), 0.0)
            weight = reach * reach * reach
            growth = approach * weight
            damping = jnp.minimum(approach, 0.0) / ((dist_sq + 0.01) * (rho[a, rows] + act_rho))
            pressing = (push[a, rows] + act_push + damping) * weight
            for place, value in ((0, pressing), (PB, growth)):
                high = value.astype(jnp.bfloat16)
                factor[slot, pl.ds(place + low, 16), 0:PB] = high
                factor[slot, pl.ds(place + low, 16), PB : 2 * PB] = (value - high.astype(jnp.float32)).astype(jnp.bfloat16)

    def second_product(k, slot):
        a = code_of(k) >> 10
        sums = lax.dot_general(
            moment[slot], factor[slot], (((1,), (1,)), ((), ())), preferred_element_type=jnp.float32
        )
        total[a, 0] += sums[0:8, 0:PB]
        total[a, 1] += sums[0:8, PB : 2 * PB]

    def one_step(step, carry):
        for slot in range(TOGETHER):
            second_product(TOGETHER * (step - 3) + slot, slot)
        for slot in range(TOGETHER):
            elementwise(TOGETHER * (step - 2) + slot, slot)
        for slot in range(TOGETHER):
            first_product(TOGETHER * (step - 1) + slot, slot)
        for slot in range(TOGETHER):
            prepare(TOGETHER * step + slot, slot)
        return carry

    lax.fori_loop(0, (number + 4 * TOGETHER - 1) // TOGETHER, one_step, 0)
    length = length_ref[0]
    elapsed = step_ref[0].astype(jnp.float32) * length
    strength = BLAST_STRENGTH * jnp.exp(jnp.full((1, PB), -elapsed / DECAY_TIME, jnp.float32))
    for block in range(BLK_DEV):
        fields = all_ref[tile * CHUNK + block]
        columns = pl.ds(block * PB, PB)
        moments = total[block, 0, 0:4] + total[block, 0, 4:8]
        growth = -(total[block, 1, 0:1] + total[block, 1, 4:5])
        relative = fields[0:3] + 1.0
        spread_sq = jnp.sum(relative * relative, axis=0, keepdims=True) + 1.0
        source = strength * relative / (spread_sq * jnp.sqrt(spread_sq))
        pushed = (fields - centre[block])[0:3] * moments[0:1] - moments[1:4]
        forcing = pushed + source
        velocity = fields[3:6] + length * forcing
        position = fields[0:3] + length * velocity
        density = fields[6:7] + length * growth
        rates_ref[:, columns] = jnp.concatenate([growth, forcing], axis=0)
        ahead_ref[:, columns] = jnp.concatenate([position, velocity, density], axis=0)


def rates_of(step_index, time_step, lists, gathered):
    smem = pl.BlockSpec(memory_space=pltpu.SMEM)
    vmem = pl.BlockSpec(memory_space=pltpu.VMEM)
    return pl.pallas_call(
        rates_kernel,
        out_shape=(
            jax.ShapeDtypeStruct((4, BLK_DEV * PB), jnp.float32),
            jax.ShapeDtypeStruct((7, BLK_DEV * PB), jnp.float32),
        ),
        in_specs=[smem, smem, vmem, vmem],
        out_specs=(vmem, vmem),
        scratch_shapes=[
            pltpu.VMEM((BLK_DEV + 1, 8, PB), jnp.float32),
            pltpu.VMEM((BLK_DEV + 1, PB, 64), jnp.bfloat16),
            pltpu.VMEM((BLK_DEV + 1, PB, PB), jnp.float32),
            pltpu.VMEM((BLK_DEV + 1, PB, PB), jnp.float32),
            pltpu.VMEM((BLK_DEV + 1, 2, 8, PB), jnp.float32),
            pltpu.VMEM((8, PB), jnp.int32),
            pltpu.VMEM((TOGETHER, 64, 2 * PB), jnp.bfloat16),
            pltpu.VMEM((TOGETHER, PB, 2 * PB), jnp.float32),
            pltpu.VMEM((TOGETHER, 2 * PB, 2 * PB), jnp.bfloat16),
            pltpu.VMEM((TOGETHER, 16, 2 * PB), jnp.bfloat16),
            pltpu.SMEM((8, PB), jnp.int32),
            pltpu.SemaphoreType.DMA,
        ],
        compiler_params=pltpu.CompilerParams(vmem_limit_bytes=16 * 2**20),
        name="tile_rates",
    )(step_index, time_step, lists, gathered)


def on_device(particles, halo_up, halo_down, tile_first, tile_second, tile_live, step_index, time_step):
    mine = jnp.transpose(particles.reshape(8, BLK_DEV, PB), (1, 0, 2))
    gathered, lists = gather(halo_up, halo_down, tile_first, tile_second, tile_live, mine)
    return rates_of(step_index, time_step, lists, gathered.reshape(N_TILE * CHUNK, 8, PB))


def solution(mesh):
    placed = (
        P(None, ("slab", "tile")),
        P(("slab", "tile")),
        P(("slab", "tile")),
        P("slab", "tile"),
        P("slab", "tile"),
        P("slab", "tile"),
        P(),
        P(),
    )
    return jax.shard_map(
        on_device,
        mesh=mesh,
        in_specs=placed,
        out_specs=(P(None, ("slab", "tile")), P(None, ("slab", "tile"))),
        check_vma=False,
    )
```

profile of v0, /device:TPU:40, one launch (start us, length us, event | category | flops | bytes accessed | tf_op | source)
XLA Modules:
  0.0 58.5 jit_solution(15705103876425349413)
XLA Ops:
  3.2 0.0 copy-start
  3.2 0.8 %copy-done = f32[8,2048]{1,0:T(8,128)S(1)} copy-done((f32[8,2048]{1,0:T(8,128)S(1)}, f32[8,2048]{1,0:T(8,128)}, u32[]{:S(2)}) %copy-start) | copy-done | bytes 65560
  4.1 0.0 copy-start.1
  4.1 0.7 %copy-done.1 = s32[1,128]{1,0:T(1,128)S(1)} copy-done((s32[1,128]{1,0:T(1,128)S(1)}, s32[1,128]{1,0:T(1,128)}, u32[]{:S(2)}) %copy-start.1) | copy-done | bytes 536
  4.7 0.0 copy-start.2
  4.7 0.7 %copy-done.2 = s32[1,128]{1,0:T(1,128)S(1)} copy-done((s32[1,128]{1,0:T(1,128)S(1)}, s32[1,128]{1,0:T(1,128)}, u32[]{:S(2)}) %copy-start.2) | copy-done | bytes 536
  5.4 0.0 copy-start.3
  5.4 0.7 %copy-done.3 = s32[1,128]{1,0:T(1,128)S(1)} copy-done((s32[1,128]{1,0:T(1,128)S(1)}, s32[1,128]{1,0:T(1,128)}, u32[]{:S(2)}) %copy-start.3) | copy-done | bytes 536
  6.0 36.7 %gather_blocks.1 = (f32[32,18,8,128]{3,2,1,0:T(8,128)S(1)}, s32[32,4,128]{2,1,0:T(4,128)S(1)}) custom-call(s32[1]{0:T(128)S(6)} %copy.10.up_ref, s32[1]{0:T(128)S(6)} %copy.11.down_ref, s32[1,128]{1,0:T(1,128)S(1)} %copy-done.1, s32[1,128]{1,0:T(1,128)S(1)} %copy-done.2, s32[1,128]{1,0:T(1,128)S(1)} %copy-done.3, f32[16,8,128]{2,1,0:T(8,128)S(1)} %bitcast.5), custom_call_target="tpu_custom_call" | custom-call | tf_op jit(solution)/shard_map/gather_blocks/pallas_call | solution.py:184
  42.8 15.7 %tile_rates.1 = (f32[4,2048]{1,0:T(4,128)}, f32[7,2048]{1,0:T(8,128)}) custom-call(s32[1]{0:T(128)S(6)} %copy.12.step_ref, f32[1]{0:T(128)S(6)} %copy.13.length_ref, s32[32,4,128]{2,1,0:T(4,128)S(1)} %get-tuple-element.4.lists_ref, f32[576,8,128]{2,1,0:T(8,128)S(1)} %bitcast.4), custom_call_target="tpu_custom_call" | custom-call | tf_op jit(solution)/shard_map/tile_rates/pallas_call | solution.py:405
Async XLA Ops:
  3.2 0.8 %copy-start = (f32[8,2048]{1,0:T(8,128)S(1)}, f32[8,2048]{1,0:T(8,128)}, u32[]{:S(2)}) copy-start(f32[8,2048]{1,0:T(8,128)} %param.8) | copy-start | bytes 196612
  4.1 0.7 %copy-start.1 = (s32[1,128]{1,0:T(1,128)S(1)}, s32[1,128]{1,0:T(1,128)}, u32[]{:S(2)}) copy-start(s32[1,128]{1,0:T(1,128)} %first_ref.1) | copy-start | bytes 1540
  4.7 0.7 %copy-start.2 = (s32[1,128]{1,0:T(1,128)S(1)}, s32[1,128]{1,0:T(1,128)}, u32[]{:S(2)}) copy-start(s32[1,128]{1,0:T(1,128)} %second_ref.1) | copy-start | bytes 1540
  5.4 0.7 %copy-start.3 = (s32[1,128]{1,0:T(1,128)S(1)}, s32[1,128]{1,0:T(1,128)}, u32[]{:S(2)}) copy-start(s32[1,128]{1,0:T(1,128)} %live_ref.1) | copy-start | bytes 1540
where the time goes:
time: 59.1 us; the launch traced here: 58.5 us
  Pallas kernels  52.4 us (89%)
  between operations  3.23 us (5%)
  local copies, waits for them, and re-layouts  2.8 us (5%)
    pallas_call x1, Pallas kernels, gather(): pl.pallas_call(gather_kernel, out_shape=(jax.ShapeDtypeStruct((N_TILE, CH...  36.7 us
    pallas_call x1, Pallas kernels, rates_of(): pl.pallas_call(rates_kernel, out_shape=(jax.ShapeDtypeStruct((4, BLK_DEV...  15.7 us
    unnamed x8, local copies, waits for them, and re-layouts  2.8 us

commit v1 on v0

--- a/solution.py
+++ b/solution.py
@@ -13,7 +13,8 @@
 N_SLAB = 16
 X, Z = 4, 8
 N_TILE = X * Z
-CHUNK = BLK_DEV + 2
+CHUNK = 1 + BLK_DEV + 2
+NO_TILE = BLK_DEV * 1024
 
 SMOOTHING = 1.0
 KERNEL_NORM = 21.0 / (16.0 * 3.141592653589793)
@@ -26,14 +27,13 @@
 MESH = pl.DeviceIdType.MESH
 
 PARTS = (
-    dict(first="z", x2="+", z4="+", lo=0, hi=0, at=0.0),
-    dict(first="z", x2="+", z4="+", lo=0, hi=6, at=0.1),
-    dict(first="x", x2="+", z4="+", lo=6, hi=10, at=0.1),
-    dict(first="z", x2="-", z4="-", lo=10, hi=15, at=0.2),
-    dict(first="x", x2="-", z4="-", lo=15, hi=18, at=2.0),
+    dict(first="x", x2="+", z4="+", lo=7, hi=11, at=0.0),
+    dict(first="z", x2="-", z4="-", lo=11, hi=16, at=0.1),
+    dict(first="z", x2="+", z4="+", lo=0, hi=7, at=0.4),
+    dict(first="x", x2="-", z4="-", lo=16, hi=19, at=1.9),
 )
 BLOCK_US = 4096 / 46.5e3
-HOP_US = 1.66
+HOP_US = 2.0
 
 
 def tree(part):
@@ -68,7 +68,7 @@
         now, _, index, node = heapq.heappop(events)
         sends = sorted(trees[index].get(node, []), key=lambda item: -depth(index, item[1]))
         steps.append((index, node, sends))
-        blocks = PARTS[index]["hi"] - PARTS[index]["lo"] or 0.5
+        blocks = PARTS[index]["hi"] - PARTS[index]["lo"]
         for way, child in sends:
             done = max(now, free[way]) + blocks * BLOCK_US
             free[way] = done
@@ -77,11 +77,13 @@
 
 
 STEPS = schedule()
+LEAVES = {(index, node) for index, node, sends in STEPS if not sends}
+EARLY = 8
 
 
 def gather_kernel(up_ref, down_ref, first_ref, second_ref, live_ref, mine_ref,
-                  all_ref, lists_ref,
-                  own, rim, slots, tiles, slots_sem, own_sem, place_sem, tiles_sem, rim_send, rim_recv, send_sem, recv_sem):
+                  all_ref, codes_ref, centre_ref, left_ref, push_ref, rho_ref,
+                  own, rim, slots, fetch_sem, rim_send, rim_recv, send_sem, recv_sem, leaf_sem):
     slab = lax.axis_index("slab")
     tile = lax.axis_index("tile")
     x, z = tile // Z, tile % Z
@@ -93,14 +95,21 @@
         "z+": x * Z + lax.rem(z + 1, Z),
         "z-": x * Z + lax.rem(z + Z - 1, Z),
     }
-    load = pltpu.make_async_copy(mine_ref, own, own_sem)
-    load.start()
+    row = iota((8, PB), 0)
+
+    def held(origin, low, high):
+        return all_ref.at[pl.ds(origin * CHUNK + low, high - low)]
+
+    place = pltpu.make_async_copy(mine_ref, held(tile, 1, 1 + BLK_DEV), fetch_sem.at[0])
+    load = pltpu.make_async_copy(mine_ref, own, fetch_sem.at[1])
     fetch = [
-        pltpu.make_async_copy(ref, slots.at[place], slots_sem.at[place])
-        for place, ref in enumerate((first_ref, second_ref, live_ref))
+        pltpu.make_async_copy(ref, slots.at[index], fetch_sem.at[2 + index])
+        for index, ref in enumerate((first_ref, second_ref, live_ref))
     ]
+    place.start()
     for copy in fetch:
         copy.start()
+    load.start()
     barrier = pltpu.get_barrier_semaphore()
     for way in beside:
         pl.semaphore_signal(barrier, inc=1, device_id=(slab, beside[way]), device_id_type=MESH)
@@ -108,118 +117,137 @@
     pl.semaphore_signal(barrier, inc=1, device_id=(below, tile), device_id_type=MESH)
     for copy in fetch:
         copy.wait()
-    tiles[...] = jnp.concatenate([slots[0], slots[1], slots[2], jnp.zeros((1, PB), jnp.int32)], axis=0)
+    all_ref[tile * CHUNK] = jnp.where(
+        row == 0, slots[0], jnp.where(row == 1, slots[1], jnp.where(row == 2, slots[2], 0))
+    ).astype(jnp.float32)
     load.wait()
     rim[0] = own[up_ref[0]]
     rim[1] = own[down_ref[0]]
-    place = pltpu.make_async_copy(own, all_ref.at[tile, pl.ds(0, BLK_DEV)], place_sem)
-    place.start()
-    mark = pltpu.make_async_copy(tiles, lists_ref.at[tile], tiles_sem)
-    mark.start()
+    place.wait()
     pl.semaphore_wait(barrier, 6)
 
     def rim_copy(side):
         return pltpu.make_async_remote_copy(
-            src_ref=rim.at[side],
-            dst_ref=all_ref.at[tile, BLK_DEV + side],
+            src_ref=rim.at[pl.ds(side, 1)],
+            dst_ref=held(tile, 1 + BLK_DEV + side, 2 + BLK_DEV + side),
             send_sem=rim_send.at[side],
             recv_sem=rim_recv.at[side],
             device_id=(above if side == 0 else below, tile),
             device_id_type=MESH,
         )
 
+    def pass_on(where, signal, way):
+        return pltpu.make_async_remote_copy(
+            src_ref=where,
+            dst_ref=where,
+            send_sem=send_sem,
+            recv_sem=signal,
+            device_id=(slab, beside[way]),
+            device_id_type=MESH,
+        )
+
+    def piece(index, node):
+        origin = lax.rem(x + X - node[0], X) * Z + lax.rem(z + Z - node[1], Z)
+        return held(origin, PARTS[index]["lo"], PARTS[index]["hi"])
+
+    def arrival(index, node):
+        if (index, node) in LEAVES:
+            return leaf_sem.at[0 if PARTS[index]["lo"] == 0 else 1]
+        return recv_sem.at[index * N_TILE + node[0] * Z + node[1]]
+
+    def one_pair(pair, carry):
+        for block in (2 * pair, 2 * pair + 1):
+            middle, side = receiver(own[block], row)
+            centre_ref[block] = middle
+            left_ref[block] = side.astype(jnp.bfloat16)
+            push_ref[block] = jnp.broadcast_to(side[:, 56:57], (PB, PB))
+            rho_ref[block] = jnp.broadcast_to(side[:, 57:58], (PB, PB))
+        return carry
+
     rims = [rim_copy(0), rim_copy(1)]
     for copy in rims:
         copy.start()
-    place.wait()
-    mark.wait()
-
-    def piece(index, node):
-        origin = lax.rem(x + X - node[0], X) * Z + lax.rem(z + Z - node[1], Z)
-        if index == 0:
-            return lists_ref.at[origin]
-        part = PARTS[index]
-        return all_ref.at[origin, pl.ds(part["lo"], part["hi"] - part["lo"])]
-
-    def slot(index, node):
-        return index * N_TILE + node[0] * Z + node[1]
-
-    sent = []
+    started = 0
     for index, node, sends in STEPS:
-        held = piece(index, node)
+        if (index, node) in LEAVES:
+            continue
+        where = piece(index, node)
         if node != (0, 0):
-            pltpu.make_async_remote_copy(
-                src_ref=held,
-                dst_ref=held,
-                send_sem=send_sem.at[slot(index, node)],
-                recv_sem=recv_sem.at[slot(index, node)],
-                device_id=(slab, beside["x+"]),
-                device_id_type=MESH,
-            ).wait_recv()
-        elif PARTS[index]["hi"] > BLK_DEV:
+            pass_on(where, arrival(index, node), "x+").wait_recv()
+        elif PARTS[index]["hi"] == CHUNK:
+            lax.fori_loop(0, EARLY // 2, one_pair, 0)
             for copy in rims:
                 copy.wait_recv()
         for way, child in sends:
-            copy = pltpu.make_async_remote_copy(
-                src_ref=held,
-                dst_ref=held,
-                send_sem=send_sem.at[slot(index, child)],
-                recv_sem=recv_sem.at[slot(index, child)],
-                device_id=(slab, beside[way]),
-                device_id_type=MESH,
-            )
-            copy.start()
-            sent.append(copy)
+            pass_on(where, arrival(index, child), way).start()
+    lax.fori_loop(EARLY // 2, BLK_DEV // 2, one_pair, 0)
+    centre_ref[BLK_DEV] = jnp.zeros((8, PB), jnp.float32)
+    left_ref[BLK_DEV] = jnp.zeros((PB, 64), jnp.bfloat16)
+    push_ref[BLK_DEV] = jnp.zeros((PB, PB), jnp.float32)
+    rho_ref[BLK_DEV] = jnp.full((PB, PB), -1.0, jnp.float32)
+    listed, other = (sum(PARTS[index]["hi"] - PARTS[index]["lo"] for index, _ in LEAVES
+                         if (PARTS[index]["lo"] == 0) == first) for first in (True, False))
+    pass_on(all_ref.at[pl.ds(0, listed)], leaf_sem.at[0], "x+").wait_recv()
+    codes_ref[...] = choose_tiles(all_ref, slab, tile)
+    pass_on(all_ref.at[pl.ds(0, other)], leaf_sem.at[1], "x+").wait_recv()
     for copy in rims:
         copy.wait_send()
-    for copy in sent:
-        copy.wait_send()
+    pass_on(all_ref.at[pl.ds(0, (N_TILE - 1) * CHUNK)], leaf_sem.at[0], "x+").wait_send()
 
 
 def gather(halo_up, halo_down, tile_first, tile_second, tile_live, mine):
     smem = pl.BlockSpec(memory_space=pltpu.SMEM)
     hbm = pl.BlockSpec(memory_space=pltpu.HBM)
-    anywhere = pl.BlockSpec(memory_space=pl.ANY)
-    slots = len(PARTS) * N_TILE
+    vmem = pl.BlockSpec(memory_space=pltpu.VMEM)
+    in_hbm = [
+        pltpu.with_memory_space_constraint(array, pltpu.HBM)
+        for array in (tile_first, tile_second, tile_live, mine)
+    ]
     return pl.pallas_call(
         gather_kernel,
         out_shape=(
-            jax.ShapeDtypeStruct((N_TILE, CHUNK, 8, PB), jnp.float32),
-            jax.ShapeDtypeStruct((N_TILE, 4, PB), jnp.int32),
+            jax.ShapeDtypeStruct((N_TILE * CHUNK, 8, PB), jnp.float32),
+            jax.ShapeDtypeStruct((8, PB), jnp.int32),
+            jax.ShapeDtypeStruct((BLK_DEV + 1, 8, PB), jnp.float32),
+            jax.ShapeDtypeStruct((BLK_DEV + 1, PB, 64), jnp.bfloat16),
+            jax.ShapeDtypeStruct((BLK_DEV + 1, PB, PB), jnp.float32),
+            jax.ShapeDtypeStruct((BLK_DEV + 1, PB, PB), jnp.float32),
         ),
         in_specs=[smem, smem, hbm, hbm, hbm, hbm],
-        out_specs=(anywhere, anywhere),
+        out_specs=(vmem,) * 6,
         scratch_shapes=[
             pltpu.VMEM((BLK_DEV, 8, PB), jnp.float32),
             pltpu.VMEM((2, 8, PB), jnp.float32),
             pltpu.VMEM((3, 1, PB), jnp.int32),
-            pltpu.VMEM((4, PB), jnp.int32),
-            pltpu.SemaphoreType.DMA((3,)),
-            pltpu.SemaphoreType.DMA,
-            pltpu.SemaphoreType.DMA,
-            pltpu.SemaphoreType.DMA,
+            pltpu.SemaphoreType.DMA((5,)),
             pltpu.SemaphoreType.DMA((2,)),
             pltpu.SemaphoreType.DMA((2,)),
-            pltpu.SemaphoreType.DMA((slots,)),
-            pltpu.SemaphoreType.DMA((slots,)),
+            pltpu.SemaphoreType.DMA,
+            pltpu.SemaphoreType.DMA((len(PARTS) * N_TILE,)),
+            pltpu.SemaphoreType.DMA((2,)),
         ],
-        compiler_params=pltpu.CompilerParams(collective_id=0, has_side_effects=True, vmem_limit_bytes=4 * 2**20),
+        compiler_params=pltpu.CompilerParams(collective_id=0, has_side_effects=True, vmem_limit_bytes=16 * 2**20),
         name="gather_blocks",
-    )(halo_up, halo_down, tile_first, tile_second, tile_live, mine)
+    )(halo_up, halo_down, *in_hbm)
 
 
 def iota(shape, axis):
     return lax.broadcasted_iota(jnp.int32, shape, axis)
 
 
-def choose_tiles(lists, slab, tile):
-    first, second, live = lists[:, 0, :], lists[:, 1, :], lists[:, 2, :]
+def choose_tiles(all_ref, slab, tile):
+    first, second, live = (
+        jnp.concatenate(
+            [all_ref[origin * CHUNK, pl.ds(place, 1)] for origin in range(N_TILE)], axis=0
+        ).astype(jnp.int32)
+        for place in range(3)
+    )
     missing = ((slab == 0) & (second >= 512) & (second < 544)) | ((slab == N_SLAB - 1) & (second >= 544))
     wanted = ((first >> 4) == tile) & (live == 1) & jnp.logical_not(missing)
     source = jnp.where(
         second < 512,
-        (second >> 4) * CHUNK + (second & 15),
-        ((second - 512) & 31) * CHUNK + BLK_DEV + ((second - 512) >> 5),
+        (second >> 4) * CHUNK + 1 + (second & 15),
+        ((second - 512) & 31) * CHUNK + 1 + BLK_DEV + ((second - 512) >> 5),
     )
     code = ((first & 15) * 1024 + source).astype(jnp.float32)
     ones = jnp.where(wanted, 1.0, 0.0)
@@ -237,7 +265,9 @@
         precision=lax.Precision.HIGHEST, preferred_element_type=jnp.float32,
     )
     count = jnp.sum(before[N_TILE - 1 :, :] + within[N_TILE - 1 :, PB - 1 :])
-    return jnp.where(iota((8, PB), 0) == 0, codes, count).astype(jnp.int32)
+    row = iota((8, PB), 0)
+    codes = jnp.where((row == 0) & (iota((8, PB), 1).astype(jnp.float32) < count), codes, float(NO_TILE))
+    return jnp.where(row == 2, count, codes).astype(jnp.int32)
 
 
 def shifted(rows, up):
@@ -295,45 +325,26 @@
     return jnp.concatenate(sides, axis=1).astype(jnp.bfloat16)
 
 
-NO_TILE = BLK_DEV * 1024
 TOGETHER = 2
 
 
-def rates_kernel(step_ref, length_ref, lists_ref, all_ref, rates_ref, ahead_ref,
-                 centre, left, push, rho, total, codes, right, squares, factor, moment, plan, plan_sem):
-    slab = lax.axis_index("slab")
+def rates_kernel(step_ref, length_ref, codes, all_ref, centre, left, push, rho, rates_ref, ahead_ref,
+                 total, right, squares, factor, moment, plan, plan_sem):
     tile = lax.axis_index("tile")
     row = iota((8, PB), 0)
-    codes[...] = choose_tiles(lists_ref[...], slab, tile)
     copy = pltpu.make_async_copy(codes, plan, plan_sem)
     copy.start()
     total[...] = jnp.zeros_like(total)
-
-    def one_block(block, carry):
-        middle, side = receiver(all_ref[tile * CHUNK + block], row)
-        centre[block] = middle
-        left[block] = side.astype(jnp.bfloat16)
-        push[block] = jnp.broadcast_to(side[:, 56:57], (PB, PB))
-        rho[block] = jnp.broadcast_to(side[:, 57:58], (PB, PB))
-        return carry
-
-    lax.fori_loop(0, BLK_DEV, one_block, 0)
     copy.wait()
-    number = plan[1, 0]
-
-    def code_of(k):
-        code = plan[0, jnp.clip(k, 0, PB - 1)]
-        return jnp.where((k >= 0) & (k < number), code, NO_TILE)
-
-    def prepare(k, slot):
-        code = code_of(k)
+    number = plan[2, 0]
+
+    def prepare(code, slot):
         right[slot] = actor_side(all_ref[code & 1023] - centre[code >> 10], row)
 
-    def first_product(k, slot):
-        squares[slot] = jnp.dot(left[code_of(k) >> 10], right[slot], preferred_element_type=jnp.float32)
-
-    def elementwise(k, slot):
-        code = code_of(k)
+    def first_product(code, slot):
+        squares[slot] = jnp.dot(left[code >> 10], right[slot], preferred_element_type=jnp.float32)
+
+    def elementwise(code, slot):
         a = code >> 10
         fields = all_ref[code & 1023]
         centred = fields - centre[a]
@@ -359,31 +370,34 @@
                 factor[slot, pl.ds(place + low, 16), 0:PB] = high
                 factor[slot, pl.ds(place + low, 16), PB : 2 * PB] = (value - high.astype(jnp.float32)).astype(jnp.bfloat16)
 
-    def second_product(k, slot):
-        a = code_of(k) >> 10
+    def second_product(code, slot):
+        a = code >> 10
         sums = lax.dot_general(
             moment[slot], factor[slot], (((1,), (1,)), ((), ())), preferred_element_type=jnp.float32
         )
         total[a, 0] += sums[0:8, 0:PB]
         total[a, 1] += sums[0:8, PB : 2 * PB]
 
-    def one_step(step, carry):
+    def one_step(step, stages):
+        made, multiplied, weighed = stages
+        fresh = [plan[(TOGETHER * step + slot) >> 7, (TOGETHER * step + slot) & 127] for slot in range(TOGETHER)]
         for slot in range(TOGETHER):
-            second_product(TOGETHER * (step - 3) + slot, slot)
+            second_product(weighed[slot], slot)
         for slot in range(TOGETHER):
-            elementwise(TOGETHER * (step - 2) + slot, slot)
+            elementwise(multiplied[slot], slot)
         for slot in range(TOGETHER):
-            first_product(TOGETHER * (step - 1) + slot, slot)
+            first_product(made[slot], slot)
         for slot in range(TOGETHER):
-            prepare(TOGETHER * step + slot, slot)
-        return carry
-
-    lax.fori_loop(0, (number + 4 * TOGETHER - 1) // TOGETHER, one_step, 0)
+            prepare(fresh[slot], slot)
+        return fresh, made, multiplied
+
+    nothing = [jnp.int32(NO_TILE)] * TOGETHER
+    lax.fori_loop(0, (number + 4 * TOGETHER - 1) // TOGETHER, one_step, (nothing, nothing, nothing))
     length = length_ref[0]
     elapsed = step_ref[0].astype(jnp.float32) * length
     strength = BLAST_STRENGTH * jnp.exp(jnp.full((1, PB), -elapsed / DECAY_TIME, jnp.float32))
     for block in range(BLK_DEV):
-        fields = all_ref[tile * CHUNK + block]
+        fields = all_ref[tile * CHUNK + 1 + block]
         columns = pl.ds(block * PB, PB)
         moments = total[block, 0, 0:4] + total[block, 0, 4:8]
         growth = -(total[block, 1, 0:1] + total[block, 1, 4:5])
@@ -399,24 +413,20 @@
         ahead_ref[:, columns] = jnp.concatenate([position, velocity, density], axis=0)
 
 
-def rates_of(step_index, time_step, lists, gathered):
+def rates_of(step_index, time_step, gathered):
     smem = pl.BlockSpec(memory_space=pltpu.SMEM)
     vmem = pl.BlockSpec(memory_space=pltpu.VMEM)
+    all_blocks, codes, centre, left, push, rho = gathered
     return pl.pallas_call(
         rates_kernel,
         out_shape=(
             jax.ShapeDtypeStruct((4, BLK_DEV * PB), jnp.float32),
             jax.ShapeDtypeStruct((7, BLK_DEV * PB), jnp.float32),
         ),
-        in_specs=[smem, smem, vmem, vmem],
+        in_specs=[smem, smem] + [vmem] * 6,
         out_specs=(vmem, vmem),
         scratch_shapes=[
-            pltpu.VMEM((BLK_DEV + 1, 8, PB), jnp.float32),
-            pltpu.VMEM((BLK_DEV + 1, PB, 64), jnp.bfloat16),
-            pltpu.VMEM((BLK_DEV + 1, PB, PB), jnp.float32),
-            pltpu.VMEM((BLK_DEV + 1, PB, PB), jnp.float32),
             pltpu.VMEM((BLK_DEV + 1, 2, 8, PB), jnp.float32),
-            pltpu.VMEM((8, PB), jnp.int32),
             pltpu.VMEM((TOGETHER, 64, 2 * PB), jnp.bfloat16),
             pltpu.VMEM((TOGETHER, PB, 2 * PB), jnp.float32),
             pltpu.VMEM((TOGETHER, 2 * PB, 2 * PB), jnp.bfloat16),
@@ -426,13 +436,13 @@
         ],
         compiler_params=pltpu.CompilerParams(vmem_limit_bytes=16 * 2**20),
         name="tile_rates",
-    )(step_index, time_step, lists, gathered)
+    )(step_index, time_step, codes, all_blocks, centre, left, push, rho)
 
 
 def on_device(particles, halo_up, halo_down, tile_first, tile_second, tile_live, step_index, time_step):
     mine = jnp.transpose(particles.reshape(8, BLK_DEV, PB), (1, 0, 2))
-    gathered, lists = gather(halo_up, halo_down, tile_first, tile_second, tile_live, mine)
-    return rates_of(step_index, time_step, lists, gathered.reshape(N_TILE * CHUNK, 8, PB))
+    gathered = gather(halo_up, halo_down, tile_first, tile_second, tile_live, mine)
+    return rates_of(step_index, time_step, gathered)
 
 
 def solution(mesh):

time: 59.1 us -> 49.2 us (0.83)
  the two profiles are of different devices: /device:TPU:40 before, /device:TPU:2 now
where the time goes in v1:
time: 49.2 us; the launch traced here: 48.5 us
  Pallas kernels  45.3 us (92%)
  between operations  3.22 us (7%)
    pallas_call x1, Pallas kernels, gather(): pl.pallas_call(gather_kernel, out_shape=(jax.ShapeDtypeStruct((N_TILE * C...  35.9 us
    pallas_call x1, Pallas kernels, rates_of(): pl.pallas_call(rates_kernel, out_shape=(jax.ShapeDtypeStruct((4, BLK_DEV...  9.46 us

profile of v1, /device:TPU:2, one launch (start us, length us, event | category | flops | bytes accessed | tf_op | source)
XLA Modules:
  0.0 48.5 jit_solution(16755660362182755848)
XLA Ops:
  3.2 35.9 %gather_blocks.1 = (f32[608,8,128]{2,1,0:T(8,128)S(1)}, s32[8,128]{1,0:T(8,128)S(1)}, f32[17,8,128]{2,1,0:T(8,128)S(1)}, bf16[17,128,64]{2,1,0:T(8,128)(2,1)S(1)...) custom-call(s32[1]{0:T(128)S(6)} %copy.10.up_ref, s32[1]{0:T(128)S(6)} %copy.11.down_ref, s32[1,128]{1,0:T(1,128)} %first_ref.1, ...), custom_call_target="tpu_custom_call" | custom-call | tf_op jit(solution)/shard_map/gather_blocks/pallas_call | solution.py:206
  39.1 9.5 %tile_rates.1 = (f32[4,2048]{1,0:T(4,128)}, f32[7,2048]{1,0:T(8,128)}) custom-call(s32[1]{0:T(128)S(6)} %copy.12.step_ref, f32[1]{0:T(128)S(6)} %copy.13.length_ref, s32[8,128]{1,0:T(8,128)S(1)} %get-tuple-element.8.codes, f32[608,8,128]{2,1,0:T(8,128)S(1)} %get-tuple-element.9.all_ref, f32[17,8,128]{2,1,0:T(8,128)S(1)} %get-tuple-element.10.centre, ...), custom_call_target="tpu_custom_call" | custom-call | tf_op jit(solution)/shard_map/tile_rates/pallas_call | solution.py:420

commit v2 on v1

--- a/solution.py
+++ b/solution.py
@@ -325,11 +325,11 @@
     return jnp.concatenate(sides, axis=1).astype(jnp.bfloat16)
 
 
-TOGETHER = 2
+TOGETHER = 3
 
 
 def rates_kernel(step_ref, length_ref, codes, all_ref, centre, left, push, rho, rates_ref, ahead_ref,
-                 total, right, squares, factor, moment, plan, plan_sem):
+                 total, right, squares, factor, moment, acts, plan, plan_sem):
     tile = lax.axis_index("tile")
     row = iota((8, PB), 0)
     copy = pltpu.make_async_copy(codes, plan, plan_sem)
@@ -339,23 +339,26 @@
     number = plan[2, 0]
 
     def prepare(code, slot):
-        right[slot] = actor_side(all_ref[code & 1023] - centre[code >> 10], row)
-
-    def first_product(code, slot):
-        squares[slot] = jnp.dot(left[code >> 10], right[slot], preferred_element_type=jnp.float32)
-
-    def elementwise(code, slot):
-        a = code >> 10
         fields = all_ref[code & 1023]
-        centred = fields - centre[a]
-        act_push = jnp.broadcast_to(pressure_term(fields)[6:7], (16, PB))
-        act_rho = jnp.broadcast_to(-0.5 * fields[6:7], (16, PB))
+        centred = fields - centre[code >> 10]
+        right[slot] = actor_side(centred, row)
         mass = jnp.broadcast_to(fields[7:8] * (5.0 * KERNEL_NORM / 8.0), (8, PB))
         weighted = jnp.where(row == 0, 1.0, shifted(centred, 7)) * mass
         high = weighted.astype(jnp.bfloat16).astype(jnp.float32)
         both = jnp.where(row < 4, high, shifted(weighted - high, 4))
         both = jnp.concatenate([both, jnp.zeros((8, PB), jnp.float32)], axis=0).astype(jnp.bfloat16)
-        moment[slot] = jnp.concatenate([both, both], axis=1)
+        moment[0, slot] = jnp.concatenate([both, both], axis=1)
+        acts[0, slot] = jnp.where(row == 6, pressure_term(fields), -0.5 * shifted(fields, 7))
+
+    def first_product(code, slot):
+        squares[slot] = jnp.dot(left[code >> 10], right[slot], preferred_element_type=jnp.float32)
+        moment[1, slot] = moment[0, slot]
+        acts[1, slot] = acts[0, slot]
+
+    def elementwise(code, slot):
+        a = code >> 10
+        act_push = jnp.broadcast_to(acts[1, slot, 6:7], (16, PB))
+        act_rho = jnp.broadcast_to(acts[1, slot, 7:8], (16, PB))
         for low in range(0, PB, 16):
             rows = pl.ds(low, 16)
             dist_sq = jnp.maximum(squares[slot, rows, 0:PB], 1e-30)
@@ -367,20 +370,22 @@
             pressing = (push[a, rows] + act_push + damping) * weight
             for place, value in ((0, pressing), (PB, growth)):
                 high = value.astype(jnp.bfloat16)
+                lower = (value - high.astype(jnp.float32)).astype(jnp.bfloat16)
                 factor[slot, pl.ds(place + low, 16), 0:PB] = high
-                factor[slot, pl.ds(place + low, 16), PB : 2 * PB] = (value - high.astype(jnp.float32)).astype(jnp.bfloat16)
+                factor[slot, pl.ds(place + low, 16), PB : 2 * PB] = lower
+        moment[2, slot] = moment[1, slot]
 
     def second_product(code, slot):
         a = code >> 10
         sums = lax.dot_general(
-            moment[slot], factor[slot], (((1,), (1,)), ((), ())), preferred_element_type=jnp.float32
+            moment[2, slot], factor[slot], (((1,), (1,)), ((), ())), preferred_element_type=jnp.float32
         )
         total[a, 0] += sums[0:8, 0:PB]
         total[a, 1] += sums[0:8, PB : 2 * PB]
 
     def one_step(step, stages):
+        fresh = [plan[(TOGETHER * step + slot) >> 7, (TOGETHER * step + slot) & 127] for slot in range(TOGETHER)]
         made, multiplied, weighed = stages
-        fresh = [plan[(TOGETHER * step + slot) >> 7, (TOGETHER * step + slot) & 127] for slot in range(TOGETHER)]
         for slot in range(TOGETHER):
             second_product(weighed[slot], slot)
         for slot in range(TOGETHER):
@@ -430,7 +435,8 @@
             pltpu.VMEM((TOGETHER, 64, 2 * PB), jnp.bfloat16),
             pltpu.VMEM((TOGETHER, PB, 2 * PB), jnp.float32),
             pltpu.VMEM((TOGETHER, 2 * PB, 2 * PB), jnp.bfloat16),
-            pltpu.VMEM((TOGETHER, 16, 2 * PB), jnp.bfloat16),
+            pltpu.VMEM((3, TOGETHER, 16, 2 * PB), jnp.bfloat16),
+            pltpu.VMEM((2, TOGETHER, 8, PB), jnp.float32),
             pltpu.SMEM((8, PB), jnp.int32),
             pltpu.SemaphoreType.DMA,
         ],

time: 49.2 us -> 47.9 us (0.974); the launches traced: 48.5 us -> 47.9 us
  Pallas kernels: 45.3 us -> 44.6 us
    pallas_call x1, Pallas kernels: 9.46 us -> 8.77 us  [rates_of(): pl.pallas_call(rates_kernel, out_shape=(jax.ShapeDtypeStruct((4, BLK_DEV...]
where the time goes in v2:
time: 47.9 us
  Pallas kernels  44.6 us (93%)
  between operations  3.22 us (7%)
    pallas_call x1, Pallas kernels, gather(): pl.pallas_call(gather_kernel, out_shape=(jax.ShapeDtypeStruct((N_TILE * C...  35.9 us
    pallas_call x1, Pallas kernels, rates_of(): pl.pallas_call(rates_kernel, out_shape=(jax.ShapeDtypeStruct((4, BLK_DEV...  8.77 us

profile of v2, /device:TPU:2, one launch (start us, length us, event | category | flops | bytes accessed | tf_op | source)
XLA Modules:
  0.0 47.9 jit_solution(14725489962351850606)
XLA Ops:
  3.2 35.9 %gather_blocks.1 = (f32[608,8,128]{2,1,0:T(8,128)S(1)}, s32[8,128]{1,0:T(8,128)S(1)}, f32[17,8,128]{2,1,0:T(8,128)S(1)}, bf16[17,128,64]{2,1,0:T(8,128)(2,1)S(1)...) custom-call(s32[1]{0:T(128)S(6)} %copy.10.up_ref, s32[1]{0:T(128)S(6)} %copy.11.down_ref, s32[1,128]{1,0:T(1,128)} %first_ref.1, ...), custom_call_target="tpu_custom_call" | custom-call | tf_op jit(solution)/shard_map/gather_blocks/pallas_call | solution.py:206
  39.1 8.8 %tile_rates.1 = (f32[4,2048]{1,0:T(4,128)}, f32[7,2048]{1,0:T(8,128)}) custom-call(s32[1]{0:T(128)S(6)} %copy.12.step_ref, f32[1]{0:T(128)S(6)} %copy.13.length_ref, s32[8,128]{1,0:T(8,128)S(1)} %get-tuple-element.8.codes, f32[608,8,128]{2,1,0:T(8,128)S(1)} %get-tuple-element.9.all_ref, f32[17,8,128]{2,1,0:T(8,128)S(1)} %get-tuple-element.10.centre, ...), custom_call_target="tpu_custom_call" | custom-call | tf_op jit(solution)/shard_map/tile_rates/pallas_call | solution.py:425

commit v3 on v2

--- a/solution.py
+++ b/solution.py
@@ -27,13 +27,12 @@
 MESH = pl.DeviceIdType.MESH
 
 PARTS = (
-    dict(first="x", x2="+", z4="+", lo=7, hi=11, at=0.0),
-    dict(first="z", x2="-", z4="-", lo=11, hi=16, at=0.1),
+    dict(first="x", x2="+", z4="+", lo=13, hi=19, at=1.9),
+    dict(first="z", x2="-", z4="-", lo=7, hi=13, at=0.1),
     dict(first="z", x2="+", z4="+", lo=0, hi=7, at=0.4),
-    dict(first="x", x2="-", z4="-", lo=16, hi=19, at=1.9),
 )
 BLOCK_US = 4096 / 46.5e3
-HOP_US = 2.0
+HOP_US = 3.0
 
 
 def tree(part):
@@ -115,15 +114,6 @@
         pl.semaphore_signal(barrier, inc=1, device_id=(slab, beside[way]), device_id_type=MESH)
     pl.semaphore_signal(barrier, inc=1, device_id=(above, tile), device_id_type=MESH)
     pl.semaphore_signal(barrier, inc=1, device_id=(below, tile), device_id_type=MESH)
-    for copy in fetch:
-        copy.wait()
-    all_ref[tile * CHUNK] = jnp.where(
-        row == 0, slots[0], jnp.where(row == 1, slots[1], jnp.where(row == 2, slots[2], 0))
-    ).astype(jnp.float32)
-    load.wait()
-    rim[0] = own[up_ref[0]]
-    rim[1] = own[down_ref[0]]
-    place.wait()
     pl.semaphore_wait(barrier, 6)
 
     def rim_copy(side):
@@ -136,9 +126,9 @@
             device_id_type=MESH,
         )
 
-    def pass_on(where, signal, way):
+    def pass_on(where, signal, way, source=None):
         return pltpu.make_async_remote_copy(
-            src_ref=where,
+            src_ref=where if source is None else source,
             dst_ref=where,
             send_sem=send_sem,
             recv_sem=signal,
@@ -165,17 +155,35 @@
         return carry
 
     rims = [rim_copy(0), rim_copy(1)]
+    for index, node, sends in STEPS:
+        part = PARTS[index]
+        if node == (0, 0) and part["lo"] > 0 and part["hi"] <= 1 + BLK_DEV:
+            for way, child in sends:
+                source = mine_ref.at[pl.ds(part["lo"] - 1, part["hi"] - part["lo"])]
+                pass_on(piece(index, node), arrival(index, child), way, source).start()
+    for copy in fetch:
+        copy.wait()
+    all_ref[tile * CHUNK] = jnp.where(
+        row == 0, slots[0], jnp.where(row == 1, slots[1], jnp.where(row == 2, slots[2], 0))
+    ).astype(jnp.float32)
+    load.wait()
+    rim[0] = own[up_ref[0]]
+    rim[1] = own[down_ref[0]]
+    lax.fori_loop(0, 1, one_pair, 0)
     for copy in rims:
         copy.start()
-    started = 0
+    place.wait()
     for index, node, sends in STEPS:
         if (index, node) in LEAVES:
+            continue
+        part = PARTS[index]
+        if node == (0, 0) and part["lo"] > 0 and part["hi"] <= 1 + BLK_DEV:
             continue
         where = piece(index, node)
         if node != (0, 0):
             pass_on(where, arrival(index, node), "x+").wait_recv()
-        elif PARTS[index]["hi"] == CHUNK:
-            lax.fori_loop(0, EARLY // 2, one_pair, 0)
+        elif part["hi"] == CHUNK:
+            lax.fori_loop(1, EARLY // 2, one_pair, 0)
             for copy in rims:
                 copy.wait_recv()
         for way, child in sends:
@@ -383,21 +391,37 @@
         total[a, 0] += sums[0:8, 0:PB]
         total[a, 1] += sums[0:8, PB : 2 * PB]
 
+    def group(step):
+        return [plan[(TOGETHER * step + slot) >> 7, (TOGETHER * step + slot) & 127] for slot in range(TOGETHER)]
+
+    def stage(work, codes_now):
+        for slot in range(TOGETHER):
+            work(codes_now[slot], slot)
+
     def one_step(step, stages):
-        fresh = [plan[(TOGETHER * step + slot) >> 7, (TOGETHER * step + slot) & 127] for slot in range(TOGETHER)]
         made, multiplied, weighed = stages
-        for slot in range(TOGETHER):
-            second_product(weighed[slot], slot)
-        for slot in range(TOGETHER):
-            elementwise(multiplied[slot], slot)
-        for slot in range(TOGETHER):
-            first_product(made[slot], slot)
-        for slot in range(TOGETHER):
-            prepare(fresh[slot], slot)
+        fresh = group(step)
+        stage(second_product, weighed)
+        stage(elementwise, multiplied)
+        stage(first_product, made)
+        stage(prepare, fresh)
         return fresh, made, multiplied
 
-    nothing = [jnp.int32(NO_TILE)] * TOGETHER
-    lax.fori_loop(0, (number + 4 * TOGETHER - 1) // TOGETHER, one_step, (nothing, nothing, nothing))
+    one, two, three = group(0), group(1), group(2)
+    stage(prepare, one)
+    stage(first_product, one)
+    stage(prepare, two)
+    stage(elementwise, one)
+    stage(first_product, two)
+    stage(prepare, three)
+    steps = jnp.maximum((number + TOGETHER - 1) // TOGETHER, 3)
+    three, two, one = lax.fori_loop(3, steps, one_step, (three, two, one))
+    stage(second_product, one)
+    stage(elementwise, two)
+    stage(first_product, three)
+    stage(second_product, two)
+    stage(elementwise, three)
+    stage(second_product, three)
     length = length_ref[0]
     elapsed = step_ref[0].astype(jnp.float32) * length
     strength = BLAST_STRENGTH * jnp.exp(jnp.full((1, PB), -elapsed / DECAY_TIME, jnp.float32))

time: 47.9 us -> 46.5 us (0.971)
  Pallas kernels: 44.6 us -> 43 us
    pallas_call x1, Pallas kernels: 8.77 us -> 7.83 us  [rates_of(): pl.pallas_call(rates_kernel, out_shape=(jax.ShapeDtypeStruct((4, BLK_DEV...]
    pallas_call x1, Pallas kernels: 35.9 us -> 35.1 us  [gather(): pl.pallas_call(gather_kernel, out_shape=(jax.ShapeDtypeStruct((N_TILE * C...]
where the time goes in v3:
time: 46.5 us; the launch traced here: 46.2 us
  Pallas kernels  43 us (92%)
  between operations  3.22 us (7%)
    pallas_call x1, Pallas kernels, gather(): pl.pallas_call(gather_kernel, out_shape=(jax.ShapeDtypeStruct((N_TILE * C...  35.1 us
    pallas_call x1, Pallas kernels, rates_of(): pl.pallas_call(rates_kernel, out_shape=(jax.ShapeDtypeStruct((4, BLK_DEV...  7.83 us

profile of v3, /device:TPU:2, one launch (start us, length us, event | category | flops | bytes accessed | tf_op | source)
XLA Modules:
  0.0 46.2 jit_solution(16091459081882268362)
XLA Ops:
  3.2 35.1 %gather_blocks.1 = (f32[608,8,128]{2,1,0:T(8,128)S(1)}, s32[8,128]{1,0:T(8,128)S(1)}, f32[17,8,128]{2,1,0:T(8,128)S(1)}, bf16[17,128,64]{2,1,0:T(8,128)(2,1)S(1)...) custom-call(s32[1]{0:T(128)S(6)} %copy.10.up_ref, s32[1]{0:T(128)S(6)} %copy.11.down_ref, s32[1,128]{1,0:T(1,128)} %first_ref.1, ...), custom_call_target="tpu_custom_call" | custom-call | tf_op jit(solution)/shard_map/gather_blocks/pallas_call | solution.py:214
  38.3 7.8 %tile_rates.1 = (f32[4,2048]{1,0:T(4,128)}, f32[7,2048]{1,0:T(8,128)}) custom-call(s32[1]{0:T(128)S(6)} %copy.12.step_ref, f32[1]{0:T(128)S(6)} %copy.13.length_ref, s32[8,128]{1,0:T(8,128)S(1)} %get-tuple-element.8.codes, f32[608,8,128]{2,1,0:T(8,128)S(1)} %get-tuple-element.9.all_ref, f32[17,8,128]{2,1,0:T(8,128)S(1)} %get-tuple-element.10.centre, ...), custom_call_target="tpu_custom_call" | custom-call | tf_op jit(solution)/shard_map/tile_rates/pallas_call | solution.py:449

commit v4 on v3

--- a/solution.py
+++ b/solution.py
@@ -27,9 +27,9 @@
 MESH = pl.DeviceIdType.MESH
 
 PARTS = (
-    dict(first="x", x2="+", z4="+", lo=13, hi=19, at=1.9),
-    dict(first="z", x2="-", z4="-", lo=7, hi=13, at=0.1),
-    dict(first="z", x2="+", z4="+", lo=0, hi=7, at=0.4),
+    dict(first="x", x2="-", z4="-", lo=13, hi=19, at=1.9),
+    dict(first="z", x2="-", z4="+", lo=7, hi=13, at=0.1),
+    dict(first="z", x2="+", z4="-", lo=0, hi=7, at=0.4),
 )
 BLOCK_US = 4096 / 46.5e3
 HOP_US = 3.0
@@ -136,9 +136,12 @@
             device_id_type=MESH,
         )
 
+    from_x = [lax.rem(x + X - step, X) * (Z * CHUNK) for step in range(X)]
+    from_z = [lax.rem(z + Z - step, Z) * CHUNK for step in range(Z)]
+
     def piece(index, node):
-        origin = lax.rem(x + X - node[0], X) * Z + lax.rem(z + Z - node[1], Z)
-        return held(origin, PARTS[index]["lo"], PARTS[index]["hi"])
+        low, high = PARTS[index]["lo"], PARTS[index]["hi"]
+        return all_ref.at[pl.ds(from_x[node[0]] + from_z[node[1]] + low, high - low)]
 
     def arrival(index, node):
         if (index, node) in LEAVES:
@@ -267,7 +270,7 @@
     target = iota((PB, PB), 0)
     chosen = jnp.zeros((PB, PB), jnp.float32)
     for row in range(N_TILE):
-        chosen = chosen + jnp.where(place[row : row + 1, :] == target, code[row : row + 1, :], 0.0)
+        chosen = jnp.where(place[row : row + 1, :] == target, code[row : row + 1, :], chosen)
     codes = lax.dot_general(
         jnp.ones((8, PB), jnp.float32), chosen, (((1,), (1,)), ((), ())),
         precision=lax.Precision.HIGHEST, preferred_element_type=jnp.float32,

time: 46.5 us -> 45.6 us (0.981)
  the two profiles are of different devices: /device:TPU:2 before, /device:TPU:56 now
where the time goes in v4:
time: 45.6 us; the launch traced here: 45.8 us
  Pallas kernels  42.6 us (93%)
  between operations  3.22 us (7%)
    pallas_call x1, Pallas kernels, gather(): pl.pallas_call(gather_kernel, out_shape=(jax.ShapeDtypeStruct((N_TILE * C...  33.8 us
    pallas_call x1, Pallas kernels, rates_of(): pl.pallas_call(rates_kernel, out_shape=(jax.ShapeDtypeStruct((4, BLK_DEV...  8.71 us

profile of v4, /device:TPU:56, one launch (start us, length us, event | category | flops | bytes accessed | tf_op | source)
XLA Modules:
  0.0 45.8 jit_solution(6317431114721906748)
XLA Ops:
  3.2 33.8 %gather_blocks.1 = (f32[608,8,128]{2,1,0:T(8,128)S(1)}, s32[8,128]{1,0:T(8,128)S(1)}, f32[17,8,128]{2,1,0:T(8,128)S(1)}, bf16[17,128,64]{2,1,0:T(8,128)(2,1)S(1)...) custom-call(s32[1]{0:T(128)S(6)} %copy.10.up_ref, s32[1]{0:T(128)S(6)} %copy.11.down_ref, s32[1,128]{1,0:T(1,128)} %first_ref.1, ...), custom_call_target="tpu_custom_call" | custom-call | tf_op jit(solution)/shard_map/gather_blocks/pallas_call | solution.py:217
  37.1 8.7 %tile_rates.1 = (f32[4,2048]{1,0:T(4,128)}, f32[7,2048]{1,0:T(8,128)}) custom-call(s32[1]{0:T(128)S(6)} %copy.12.step_ref, f32[1]{0:T(128)S(6)} %copy.13.length_ref, s32[8,128]{1,0:T(8,128)S(1)} %get-tuple-element.8.codes, f32[608,8,128]{2,1,0:T(8,128)S(1)} %get-tuple-element.9.all_ref, f32[17,8,128]{2,1,0:T(8,128)S(1)} %get-tuple-element.10.centre, ...), custom_call_target="tpu_custom_call" | custom-call | tf_op jit(solution)/shard_map/tile_rates/pallas_call | solution.py:452

commit v5 on v4

--- a/solution.py
+++ b/solution.py
@@ -82,7 +82,7 @@
 
 def gather_kernel(up_ref, down_ref, first_ref, second_ref, live_ref, mine_ref,
                   all_ref, codes_ref, centre_ref, left_ref, push_ref, rho_ref,
-                  own, rim, slots, fetch_sem, rim_send, rim_recv, send_sem, recv_sem, leaf_sem):
+                  own, rim, slots, chosen, fetch_sem, rim_send, rim_recv, send_sem, recv_sem, leaf_sem):
     slab = lax.axis_index("slab")
     tile = lax.axis_index("tile")
     x, z = tile // Z, tile % Z
@@ -105,15 +105,15 @@
         pltpu.make_async_copy(ref, slots.at[index], fetch_sem.at[2 + index])
         for index, ref in enumerate((first_ref, second_ref, live_ref))
     ]
-    place.start()
-    for copy in fetch:
-        copy.start()
-    load.start()
     barrier = pltpu.get_barrier_semaphore()
     for way in beside:
         pl.semaphore_signal(barrier, inc=1, device_id=(slab, beside[way]), device_id_type=MESH)
     pl.semaphore_signal(barrier, inc=1, device_id=(above, tile), device_id_type=MESH)
     pl.semaphore_signal(barrier, inc=1, device_id=(below, tile), device_id_type=MESH)
+    place.start()
+    for copy in fetch:
+        copy.start()
+    load.start()
     pl.semaphore_wait(barrier, 6)
 
     def rim_copy(side):
@@ -199,8 +199,11 @@
     listed, other = (sum(PARTS[index]["hi"] - PARTS[index]["lo"] for index, _ in LEAVES
                          if (PARTS[index]["lo"] == 0) == first) for first in (True, False))
     pass_on(all_ref.at[pl.ds(0, listed)], leaf_sem.at[0], "x+").wait_recv()
-    codes_ref[...] = choose_tiles(all_ref, slab, tile)
+    chosen[...] = choose_tiles(all_ref, slab, tile)
+    hand = pltpu.make_async_copy(chosen, codes_ref, fetch_sem.at[5])
+    hand.start()
     pass_on(all_ref.at[pl.ds(0, other)], leaf_sem.at[1], "x+").wait_recv()
+    hand.wait()
     for copy in rims:
         copy.wait_send()
     pass_on(all_ref.at[pl.ds(0, (N_TILE - 1) * CHUNK)], leaf_sem.at[0], "x+").wait_send()
@@ -225,12 +228,13 @@
             jax.ShapeDtypeStruct((BLK_DEV + 1, PB, PB), jnp.float32),
         ),
         in_specs=[smem, smem, hbm, hbm, hbm, hbm],
-        out_specs=(vmem,) * 6,
+        out_specs=(vmem, pl.BlockSpec(memory_space=pltpu.SMEM)) + (vmem,) * 4,
         scratch_shapes=[
             pltpu.VMEM((BLK_DEV, 8, PB), jnp.float32),
             pltpu.VMEM((2, 8, PB), jnp.float32),
             pltpu.VMEM((3, 1, PB), jnp.int32),
-            pltpu.SemaphoreType.DMA((5,)),
+            pltpu.VMEM((8, PB), jnp.int32),
+            pltpu.SemaphoreType.DMA((6,)),
             pltpu.SemaphoreType.DMA((2,)),
             pltpu.SemaphoreType.DMA((2,)),
             pltpu.SemaphoreType.DMA,
@@ -339,14 +343,11 @@
 TOGETHER = 3
 
 
-def rates_kernel(step_ref, length_ref, codes, all_ref, centre, left, push, rho, rates_ref, ahead_ref,
-                 total, right, squares, factor, moment, acts, plan, plan_sem):
+def rates_kernel(step_ref, length_ref, plan, all_ref, centre, left, push, rho, rates_ref, ahead_ref,
+                 total, right, squares, factor, moment, acts):
     tile = lax.axis_index("tile")
     row = iota((8, PB), 0)
-    copy = pltpu.make_async_copy(codes, plan, plan_sem)
-    copy.start()
     total[...] = jnp.zeros_like(total)
-    copy.wait()
     number = plan[2, 0]
 
     def prepare(code, slot):
@@ -455,7 +456,7 @@
             jax.ShapeDtypeStruct((4, BLK_DEV * PB), jnp.float32),
             jax.ShapeDtypeStruct((7, BLK_DEV * PB), jnp.float32),
         ),
-        in_specs=[smem, smem] + [vmem] * 6,
+        in_specs=[smem, smem, smem] + [vmem] * 5,
         out_specs=(vmem, vmem),
         scratch_shapes=[
             pltpu.VMEM((BLK_DEV + 1, 2, 8, PB), jnp.float32),
@@ -464,8 +465,6 @@
             pltpu.VMEM((TOGETHER, 2 * PB, 2 * PB), jnp.bfloat16),
             pltpu.VMEM((3, TOGETHER, 16, 2 * PB), jnp.bfloat16),
             pltpu.VMEM((2, TOGETHER, 8, PB), jnp.float32),
-            pltpu.SMEM((8, PB), jnp.int32),
-            pltpu.SemaphoreType.DMA,
         ],
         compiler_params=pltpu.CompilerParams(vmem_limit_bytes=16 * 2**20),
         name="tile_rates",

time: 45.6 us -> 47.2 us (1.035)
  the two profiles are of different devices: /device:TPU:56 before, /device:TPU:2 now
where the time goes in v5:
time: 47.2 us; the launch traced here: 47.1 us
  Pallas kernels  43.9 us (93%)
  between operations  3.22 us (7%)
    pallas_call x1, Pallas kernels, gather(): pl.pallas_call(gather_kernel, out_shape=(jax.ShapeDtypeStruct((N_TILE * C...  35.8 us
    pallas_call x1, Pallas kernels, rates_of(): pl.pallas_call(rates_kernel, out_shape=(jax.ShapeDtypeStruct((4, BLK_DEV...  8.11 us

profile of v5, /device:TPU:2, one launch (start us, length us, event | category | flops | bytes accessed | tf_op | source)
XLA Modules:
  0.0 47.1 jit_solution(6412407508260626748)
XLA Ops:
  3.2 35.8 %gather_blocks.1 = (f32[608,8,128]{2,1,0:T(8,128)S(1)}, s32[8,128]{1,0:T(8,128)S(1)}, f32[17,8,128]{2,1,0:T(8,128)S(1)}, bf16[17,128,64]{2,1,0:T(8,128)(2,1)S(1)...) custom-call(s32[1]{0:T(128)S(6)} %copy.10.up_ref, s32[1]{0:T(128)S(6)} %copy.11.down_ref, s32[1,128]{1,0:T(1,128)} %first_ref.1, ...), custom_call_target="tpu_custom_call" | custom-call | tf_op jit(solution)/shard_map/gather_blocks/pallas_call | solution.py:220
  39.0 8.1 %tile_rates.1 = (f32[4,2048]{1,0:T(4,128)}, f32[7,2048]{1,0:T(8,128)}) custom-call(s32[1]{0:T(128)S(6)} %copy.12.step_ref, f32[1]{0:T(128)S(6)} %copy.13.length_ref, s32[8,128]{1,0:T(8,128)S(1)} %get-tuple-element.8.plan, f32[608,8,128]{2,1,0:T(8,128)S(1)} %get-tuple-element.9.all_ref, f32[17,8,128]{2,1,0:T(8,128)S(1)} %get-tuple-element.10.centre, ...), custom_call_target="tpu_custom_call" | custom-call | tf_op jit(solution)/shard_map/tile_rates/pallas_call | solution.py:453

commit v6 on v4

--- a/solution.py
+++ b/solution.py
@@ -105,15 +105,15 @@
         pltpu.make_async_copy(ref, slots.at[index], fetch_sem.at[2 + index])
         for index, ref in enumerate((first_ref, second_ref, live_ref))
     ]
-    place.start()
-    for copy in fetch:
-        copy.start()
-    load.start()
     barrier = pltpu.get_barrier_semaphore()
     for way in beside:
         pl.semaphore_signal(barrier, inc=1, device_id=(slab, beside[way]), device_id_type=MESH)
     pl.semaphore_signal(barrier, inc=1, device_id=(above, tile), device_id_type=MESH)
     pl.semaphore_signal(barrier, inc=1, device_id=(below, tile), device_id_type=MESH)
+    place.start()
+    for copy in fetch:
+        copy.start()
+    load.start()
     pl.semaphore_wait(barrier, 6)
 
     def rim_copy(side):

time: 45.6 us -> 45.7 us (level)
  the two profiles are of different devices: /device:TPU:56 before, /device:TPU:4 now
where the time goes in v6:
time: 45.7 us; the launch traced here: 45.4 us
  Pallas kernels  42.2 us (92%)
  between operations  3.22 us (7%)
    pallas_call x1, Pallas kernels, gather(): pl.pallas_call(gather_kernel, out_shape=(jax.ShapeDtypeStruct((N_TILE * C...  33.8 us
    pallas_call x1, Pallas kernels, rates_of(): pl.pallas_call(rates_kernel, out_shape=(jax.ShapeDtypeStruct((4, BLK_DEV...  8.42 us

profile of v6, /device:TPU:4, one launch (start us, length us, event | category | flops | bytes accessed | tf_op | source)
XLA Modules:
  0.0 45.4 jit_solution(14077464635245465879)
XLA Ops:
  3.2 33.8 %gather_blocks.1 = (f32[608,8,128]{2,1,0:T(8,128)S(1)}, s32[8,128]{1,0:T(8,128)S(1)}, f32[17,8,128]{2,1,0:T(8,128)S(1)}, bf16[17,128,64]{2,1,0:T(8,128)(2,1)S(1)...) custom-call(s32[1]{0:T(128)S(6)} %copy.10.up_ref, s32[1]{0:T(128)S(6)} %copy.11.down_ref, s32[1,128]{1,0:T(1,128)} %first_ref.1, ...), custom_call_target="tpu_custom_call" | custom-call | tf_op jit(solution)/shard_map/gather_blocks/pallas_call | solution.py:217
  37.0 8.4 %tile_rates.1 = (f32[4,2048]{1,0:T(4,128)}, f32[7,2048]{1,0:T(8,128)}) custom-call(s32[1]{0:T(128)S(6)} %copy.12.step_ref, f32[1]{0:T(128)S(6)} %copy.13.length_ref, s32[8,128]{1,0:T(8,128)S(1)} %get-tuple-element.8.codes, f32[608,8,128]{2,1,0:T(8,128)S(1)} %get-tuple-element.9.all_ref, f32[17,8,128]{2,1,0:T(8,128)S(1)} %get-tuple-element.10.centre, ...), custom_call_target="tpu_custom_call" | custom-call | tf_op jit(solution)/shard_map/tile_rates/pallas_call | solution.py:452
